TPU v7x, 128 devices: a whole 4x4x4 slice. The times are simulated.
128 devices in a mesh: leaf: 4 (over y), rows: 32 (over z, x, core).
Axes of the slice: x: 4, y: 4, z: 4, core: 2. Of those that a mesh axis runs over, the one named last changes fastest.
Arguments:
- leaf_rhs: float32 [8, 16, 2048], P(None, 'leaf', 'rows'), may hold values from -6 to 6
- parent_rhs: float32 [8, 4, 4096], P(None, 'leaf', 'rows'), may hold values from -6 to 6
- root_rhs: float32 [8, 4096], P(None, ('leaf', 'rows')), may hold values from -6 to 6
- leaf_inv: bfloat16 [16, 2048, 2048], P('leaf', 'rows'), as said below
- leaf_panel: bfloat16 [16, 8192, 2048], P('leaf', 'rows'), may hold values from -0.0625 to 0.0625
- leaf_rows: int32 [16, 8192], P('leaf', 'rows'), may hold values from 0 to 8191, as said below
- leaf_height: int32 [16], P('leaf'), may hold values from 2048 to 8192
- parent_inv: bfloat16 [4, 4096, 4096], P('leaf', 'rows'), as said below
- parent_panel: bfloat16 [4, 4096, 4096], P('leaf', 'rows'), may hold values from -0.046875 to 0.046875
- parent_rows: int32 [4, 4096], P('leaf', 'rows'), may hold values from 0 to 4095, as said below
- parent_height: int32 [4], P('leaf'), may hold values from 1024 to 4096
- root_inv: bfloat16 [4096, 4096], P('rows'), as said below
Outputs:
- leaf_solution: float32 [8, 16, 2048], P(None, 'leaf', 'rows')
- parent_solution: float32 [8, 4, 4096], P(None, 'leaf', 'rows')
- root_solution: float32 [8, 4096], P(None, ('leaf', 'rows'))
Inputs may be any that keep to these rules, and one draw needn't show every extreme that they name: `leaf_rows`: each leaf's first leaf_height entries are distinct and ascending; every entry is a valid ancestor index. `parent_rows`: each parent's first parent_height entries are distinct and ascending. `leaf_inv`: A dense well conditioned matrix. `parent_inv`: A dense well conditioned matrix. `root_inv`: A dense well conditioned matrix.
All inputs are finite; a program needn't handle non-finite values.
Results may differ from a plain program's by a relative error of at most 0.009.
Values may be sent and summed in bfloat16 or wider, within the bound.
A program may use at most 64 MiB of HBM per device.

v0:
```python
import jax
import jax.numpy as jnp
from jax import lax
from jax.sharding import PartitionSpec as P


def shards(
    leaf_rhs,
    parent_rhs,
    root_rhs,
    leaf_inv,
    leaf_panel,
    leaf_rows,
    leaf_height,
    parent_inv,
    parent_panel,
    parent_rows,
    parent_height,
    root_inv,
):
    rcount = leaf_rhs.shape[0]
    group_leaves = leaf_rhs.shape[1]
    leaf_local = leaf_panel.shape[1]
    parent_width = parent_inv.shape[2]
    root_width = root_inv.shape[1]
    row_index = lax.axis_index("rows")
    parent_cols = parent_rhs.shape[2]
    root_cols = root_rhs.shape[1]
    flat_index = lax.axis_index("leaf") * lax.axis_size("rows") + row_index
    block = leaf_inv
    ly = jnp.einsum(
        "rln,lin->rli",
        lax.all_gather(leaf_rhs.astype(jnp.bfloat16), "rows", axis=2, tiled=True),
        block,
        preferred_element_type=jnp.float32,
    )
    lyb = ly.astype(jnp.bfloat16)
    block = leaf_panel
    lupd = jnp.einsum(
        "rln,lhn->rlh",
        lax.all_gather(lyb, "rows", axis=2, tiled=True),
        block,
        preferred_element_type=jnp.float32,
    )
    leaf_pos = row_index * leaf_local + jnp.arange(leaf_local, dtype=jnp.int32)
    leaf_mask = leaf_pos[None, :] < leaf_height[:, None]
    lupd = jnp.where(leaf_mask[None, :, :], lupd, 0.0)
    leaf_flat = leaf_rows.reshape(-1)
    local_acc = (
        jnp.zeros((rcount, parent_width + root_width), jnp.float32)
        .at[:, leaf_flat]
        .add(lupd.reshape(rcount, -1))
    )
    group_acc = lax.psum(local_acc, "rows")
    parent_acc = group_acc[:, :parent_width]
    root_from_leaves = lax.psum(group_acc[:, parent_width:], "leaf")
    parent_slice = lax.dynamic_slice_in_dim(parent_acc, row_index * parent_cols, parent_cols, 1)
    prb = (parent_rhs[:, 0, :] - parent_slice).astype(jnp.bfloat16)
    inverse_rows = parent_inv[0]
    panel_rows = parent_panel[0]
    block = inverse_rows
    py = jnp.dot(
        lax.all_gather(prb, "rows", axis=1, tiled=True), block.T, preferred_element_type=jnp.float32
    )
    pyb = py.astype(jnp.bfloat16)
    parent_local = panel_rows.shape[0]
    block = panel_rows
    pupd = jnp.dot(
        lax.all_gather(pyb, "rows", axis=1, tiled=True), block.T, preferred_element_type=jnp.float32
    )
    parent_pos = row_index * parent_local + jnp.arange(parent_local, dtype=jnp.int32)
    parent_mask = parent_pos < parent_height[0]
    pupd = jnp.where(parent_mask[None, :], pupd, 0.0)
    parent_root = jnp.zeros((rcount, root_width), jnp.float32).at[:, parent_rows[0]].add(pupd)
    root_acc = root_from_leaves + lax.psum(parent_root, ("leaf", "rows"))
    root_slice = lax.dynamic_slice_in_dim(root_acc, flat_index * root_cols, root_cols, 1)
    rrb = (root_rhs - root_slice).astype(jnp.bfloat16)
    block = root_inv
    ry = jnp.dot(
        lax.all_gather(rrb, ("leaf", "rows"), axis=1, tiled=True),
        block.T,
        preferred_element_type=jnp.float32,
    )
    root_term = jnp.dot(ry.astype(jnp.bfloat16), root_inv, preferred_element_type=jnp.float32)
    root_full = lax.psum(root_term, "rows")
    root_solution = lax.dynamic_slice_in_dim(root_full, flat_index * root_cols, root_cols, 1)
    rxb = root_full.astype(jnp.bfloat16)
    parent_anc = rxb[:, parent_rows[0]]
    parent_anc = jnp.where(parent_mask[None, :], parent_anc, jnp.zeros_like(parent_anc))
    parent_term = jnp.dot(parent_anc, panel_rows, preferred_element_type=jnp.float32)
    parent_tail = lax.psum_scatter(parent_term, "rows", scatter_dimension=1, tiled=True)
    pvb = (py - parent_tail).astype(jnp.bfloat16)
    parent_sol_term = jnp.dot(pvb, inverse_rows, preferred_element_type=jnp.float32)
    parent_sol = lax.psum_scatter(parent_sol_term, "rows", scatter_dimension=1, tiled=True)
    parent_whole = lax.all_gather(parent_sol.astype(jnp.bfloat16), "rows", axis=1, tiled=True)
    ancestors = jnp.concatenate([parent_whole, rxb], axis=1)
    leaf_anc = ancestors[:, leaf_flat].reshape(rcount, group_leaves, leaf_local)
    leaf_anc = jnp.where(leaf_mask[None, :, :], leaf_anc, jnp.zeros_like(leaf_anc))
    leaf_term = jnp.einsum("rlh,lhc->rlc", leaf_anc, leaf_panel, preferred_element_type=jnp.float32)
    leaf_tail = lax.psum_scatter(leaf_term, "rows", scatter_dimension=2, tiled=True)
    lvb = (ly - leaf_tail).astype(jnp.bfloat16)
    leaf_sol_term = jnp.einsum("rli,lic->rlc", lvb, leaf_inv, preferred_element_type=jnp.float32)
    leaf_sol = lax.psum_scatter(leaf_sol_term, "rows", scatter_dimension=2, tiled=True)
    return (leaf_sol, parent_sol[:, None, :], root_solution)


def solution(mesh):
    return jax.shard_map(
        shards,
        mesh=mesh,
        in_specs=(
            P(None, "leaf", "rows"),
            P(None, "leaf", "rows"),
            P(None, ("leaf", "rows")),
            P("leaf", "rows", None),
            P("leaf", "rows", None),
            P("leaf", "rows"),
            P("leaf"),
            P("leaf", "rows", None),
            P("leaf", "rows", None),
            P("leaf", "rows"),
            P("leaf"),
            P("rows", None),
        ),
        out_specs=(P(None, "leaf", "rows"), P(None, "leaf", "rows"), P(None, ("leaf", "rows"))),
        check_vma=False,
    )
```

profile of v0, /device:TPU:0, one launch (start us, length us, event | category | flops | bytes accessed | tf_op | source)
XLA Modules:
  0.0 916.0 jit_solution(10626270217796478974)
XLA Ops:
  8.9 27.5 %all_gather.18 = bf16[8,4,2048]{0,1,2:T(4,128)(2,1)S(1)} all-gather(bf16[8,4,64]{0,1,2:T(4,128)(2,1)S(1)} %copy.62), channel_id=1, replica_groups=mesh['leaf'=4,'rows'=32] {'rows'}, dimensions={2}, use_global_device_ids=true | all-gather | bytes 135168 | tf_op jit(solution)/shard_map/all_gather | solution.py:33
  37.3 25.3 %all_gather.19 = bf16[8,4,2048]{0,1,2:T(4,128)(2,1)S(1)} all-gather(bf16[8,4,64]{0,1,2:T(4,128)(2,1)S(1)} %copy.64), channel_id=1, replica_groups=mesh['leaf'=4,'rows'=32] {'rows'}, dimensions={2}, use_global_device_ids=true | all-gather | bytes 135168 | tf_op jit(solution)/shard_map/all_gather | solution.py:41
  62.7 3.4 fusion.6
  66.3 8.2 scatter_custom_fusion
  74.5 3.5 copy.67
  78.9 100.7 %all-reduce.5.cloned.1.call-done = f32[8,8192]{1,0:T(8,128)} async-done(((f32[8,8192]{1,0:T(8,128)}), f32[8,8192]{1,0:T(8,128)}) %all-reduce.5.cloned.1.call-update) | async-done | bytes 262160 | tf_op jit(solution)/shard_map/psum | solution.py:54
  179.6 1.6 fusion.35
  181.2 24.6 %all_gather.20 = bf16[8,4096]{1,0:T(8,128)(2,1)S(1)} all-gather(bf16[8,128]{1,0:T(8,128)(2,1)S(1)} %subtract_convert_fusion.3), channel_id=1, replica_groups=mesh['leaf'=4,'rows'=32] {'rows'}, dimensions={1}, use_global_device_ids=true | all-gather | bytes 67584 | tf_op jit(solution)/shard_map/all_gather | solution.py:63
  206.2 21.5 %all_gather.21 = bf16[8,4096]{1,0:T(8,128)(2,1)S(1)} all-gather(bf16[8,128]{1,0:T(8,128)(2,1)S(1)} %get-tuple-element.22), channel_id=1, replica_groups=mesh['leaf'=4,'rows'=32] {'rows'}, dimensions={1}, use_global_device_ids=true | all-gather | bytes 67584 | tf_op jit(solution)/shard_map/all_gather | solution.py:69
  228.3 1.5 scatter_custom_fusion.1
  229.8 1.2 copy.69
  231.8 141.0 %all-reduce.9.cloned.1.call-done = f32[8,4096]{1,0:T(8,128)} async-done(((f32[8,4096]{1,0:T(8,128)}), f32[8,4096]{1,0:T(8,128)}) %all-reduce.9.cloned.1.call-update) | async-done | bytes 131088 | tf_op jit(solution)/shard_map/psum | solution.py:75
  372.8 41.1 %all-reduce.7.cloned.1.call-done = f32[8,4096]{1,0:T(8,128)} async-done(((f32[8,4096]{1,0:T(8,128)}), f32[8,4096]{1,0:T(8,128)}) %all-reduce.7.cloned.1.call-update) | async-done | bytes 131088 | tf_op jit(solution)/shard_map/psum | solution.py:56
  414.7 35.9 %all-gather = bf16[128,32,8]{1,2,0:T(8,128)(2,1)S(1)} all-gather(bf16[1,32,8]{1,2,0:T(8,128)(2,1)S(1)} %fusion.31), channel_id=1, replica_groups=mesh['leaf'=4,'rows'=32] {'leaf','rows'}, dimensions={0}, use_global_device_ids=true | all-gather | bytes 66048 | tf_op jit(solution)/shard_map/all_gather | solution.py:80
  450.9 3.2 fusion.13
  454.2 98.7 %all-reduce.11.cloned.1.call-done = f32[8,4096]{1,0:T(8,128)} async-done(((f32[8,4096]{1,0:T(8,128)}), f32[8,4096]{1,0:T(8,128)}) %all-reduce.11.cloned.1.call-update) | async-done | bytes 131088 | tf_op jit(solution)/shard_map/psum | solution.py:85
  553.8 1.3 copy.71
  555.1 2.0 gather_fusion
  557.1 1.0 fusion.14
  558.2 71.9 %reduce-scatter.9.cloned.1.call-done = f32[8,128]{1,0:T(8,128)} async-done(((f32[8,4096]{1,0:T(8,128)}), f32[8,128]{1,0:T(8,128)}) %reduce-scatter.9.cloned.1.call-update) | async-done | bytes 4112 | tf_op jit(solution)/shard_map/reduce_scatter | solution.py:91
  630.1 1.6 fusion.17
  631.7 73.8 %reduce-scatter.11.cloned.1.call-done = f32[8,128]{1,0:T(8,128)} async-done(((f32[8,4096]{1,0:T(8,128)}), f32[8,128]{1,0:T(8,128)}) %reduce-scatter.11.cloned.1.call-update) | async-done | bytes 4112 | tf_op jit(solution)/shard_map/reduce_scatter | solution.py:94
  706.2 23.5 %all_gather.23 = bf16[8,4096]{1,0:T(8,128)(2,1)S(1)} all-gather(bf16[8,128]{1,0:T(8,128)(2,1)S(1)} %convert_element_type.38), channel_id=1, replica_groups=mesh['leaf'=4,'rows'=32] {'rows'}, dimensions={1}, use_global_device_ids=true | all-gather | bytes 67584 | tf_op jit(solution)/shard_map/all_gather | solution.py:95
  730.7 3.2 gather_fusion.1
  734.1 2.8 convolution_bitcast_fusion.1
  736.9 3.1 copy.76
  740.0 4.5 reshape.143
  744.6 76.7 %reduce-scatter.13.cloned.1.call-done = f32[64,32]{1,0:T(8,128)} async-done(((f32[2048,32]{1,0:T(8,128)}), f32[64,32]{1,0:T(8,128)}) %reduce-scatter.13.cloned.1.call-update) | async-done | bytes 8208
  822.6 3.1 copy.78
  825.6 4.5 reshape.145
  830.2 1.3 constant_dynamic-slice_fusion
  831.6 76.0 %reduce-scatter.15.cloned.1.call-done = f32[64,32]{1,0:T(8,128)} async-done(((f32[2048,32]{1,0:T(8,128)}), f32[64,32]{1,0:T(8,128)}) %reduce-scatter.15.cloned.1.call-update) | async-done | bytes 8208
  (64 shorter events, 11.5 us)
Async XLA Ops:
  7.2 29.2 %copy-start = (bf16[4,64,2048]{2,1,0:T(8,128)(2,1)S(1)}, bf16[4,64,2048]{2,1,0:T(8,128)(2,1)}, u32[]{:S(2)}) copy-start(bf16[4,64,2048]{2,1,0:T(8,128)(2,1)} %param.15) | copy-start | bytes 3145732
  7.2 172.4 %all-reduce.5.cloned.1.call-start = ((), (), s32[]{:S(2)}) async-start(), calls=%async_computation.4 | async-start | bytes 524288 | tf_op jit(solution)/shard_map/psum | solution.py:54
  36.3 26.3 %copy-start.7 = (s32[4]{0:T(128)S(1)}, s32[4]{0:T(128)}, u32[]{:S(2)}) copy-start(s32[4]{0:T(128)} %param.18) | copy-start | bytes 52
  74.5 3.6 copy-start.8
  74.5 106.7 %copy-start.5 = (f32[8,1,128]{2,1,0:T(1,128)S(1)}, f32[8,1,128]{2,1,0:T(1,128)}, u32[]{:S(2)}) copy-start(f32[8,1,128]{2,1,0:T(1,128)} %param.13) | copy-start | bytes 12292
  74.5 131.4 %copy-start.3 = (bf16[1,128,4096]{2,1,0:T(8,128)(2,1)S(1)}, bf16[1,128,4096]{2,1,0:T(8,128)(2,1)}, u32[]{:S(2)}) copy-start(bf16[1,128,4096]{2,1,0:T(8,128)(2,1)} %param.19) | copy-start | bytes 3145732
  78.0 149.7 %copy-start.1 = (bf16[1,128,4096]{2,1,0:T(8,128)(2,1)S(1)}, bf16[1,128,4096]{2,1,0:T(8,128)(2,1)}, u32[]{:S(2)}) copy-start(bf16[1,128,4096]{2,1,0:T(8,128)(2,1)} %param.20) | copy-start | bytes 3145732
  78.1 294.8 %all-reduce.9.cloned.1.call-start = ((), (), s32[]{:S(2)}) async-start(), calls=%async_computation.6 | async-start | bytes 262144 | tf_op jit(solution)/shard_map/psum | solution.py:75
  228.2 185.7 %copy-start.6 = (f32[8,32]{1,0:T(8,128)S(1)}, f32[8,32]{1,0:T(8,128)}, u32[]{:S(2)}) copy-start(f32[8,32]{1,0:T(8,128)} %param.14) | copy-start | bytes 3076
  231.0 182.9 %all-reduce.7.cloned.1.call-start = ((), (), s32[]{:S(2)}) async-start(), calls=%async_computation.5 | async-start | bytes 262144 | tf_op jit(solution)/shard_map/psum | solution.py:56
  231.8 321.1 %all-reduce.11.cloned.1.call-start = ((), (), s32[]{:S(2)}) async-start(), calls=%async_computation.7 | async-start | bytes 262144 | tf_op jit(solution)/shard_map/psum | solution.py:85
  450.6 106.5 %copy-start.2 = (bf16[1,128,4096]{2,1,0:T(8,128)(2,1)S(1)}, bf16[1,128,4096]{2,1,0:T(8,128)(2,1)}, u32[]{:S(2)}) copy-start(bf16[1,128,4096]{2,1,0:T(8,128)(2,1)} %param.20) | copy-start | bytes 3145732
  450.9 179.2 %copy-start.4 = (bf16[1,128,4096]{2,1,0:T(8,128)(2,1)S(1)}, bf16[1,128,4096]{2,1,0:T(8,128)(2,1)}, u32[]{:S(2)}) copy-start(bf16[1,128,4096]{2,1,0:T(8,128)(2,1)} %param.19) | copy-start | bytes 3145732
  454.1 176.0 %reduce-scatter.9.cloned.1.call-start = ((), (), s32[]{:S(2)}) async-start(), calls=%async_computation.8 | async-start | bytes 135168 | tf_op jit(solution)/shard_map/reduce_scatter | solution.py:91
  558.1 147.3 %reduce-scatter.11.cloned.1.call-start = ((), (), s32[]{:S(2)}) async-start(), calls=%async_computation.9 | async-start | bytes 135168 | tf_op jit(solution)/shard_map/reduce_scatter | solution.py:94
  631.7 189.7 %reduce-scatter.13.cloned.1.call-start = ((), (), s32[]{:S(2)}) async-start(), calls=%async_computation.10 | async-start | bytes 1081344
  744.6 163.0 %reduce-scatter.15.cloned.1.call-start = ((), (), s32[]{:S(2)}) async-start(), calls=%async_computation.11 | async-start | bytes 1081344
Sparse Core Ops, SparseCore 0:
  78.2 101.3 all-reduce.4
  231.2 141.6 all-reduce.8
  375.1 38.7 all-reduce.6
  454.2 98.5 all-reduce.10
  558.3 71.7 reduce-scatter.8
  633.9 71.5 reduce-scatter.10
  744.7 76.6 reduce-scatter.12
  830.3 77.2 reduce-scatter.14
where the time goes:
time: 917 us; the launch traced here: 916 us
  waiting for transfers between devices  681 us (74%)
  blocking collectives  158 us (17%)
  local copies, waits for them, and re-layouts  35.6 us (4%)
  between operations  15 us (2%)
  matrix products  13.8 us (2%)
  other arithmetic  12.2 us (1%)
    unnamed x10, waiting for transfers between devices  154 us
    psum x1, waiting for transfers between devices, shards(): root_acc = root_from_leaves + lax.psum(parent_root, ('leaf', 'rows'))  141 us
    psum x1, waiting for transfers between devices, shards(): group_acc = lax.psum(local_acc, 'rows')  101 us
    psum x1, waiting for transfers between devices, shards(): root_full = lax.psum(root_term, 'rows')  98.7 us
    reduce_scatter x1, waiting for transfers between devices, shards(): lax.psum_scatter(parent_sol_term, 'rows', scatter_dimension=1, tiled=True)  73.8 us
    reduce_scatter x1, waiting for transfers between devices, shards(): lax.psum_scatter(parent_term, 'rows', scatter_dimension=1, tiled=True)  71.9 us
    psum x1, waiting for transfers between devices, shards(): root_from_leaves = lax.psum(group_acc[:, parent_width:], 'leaf')  41.1 us
    all_gather x1, blocking collectives, shards(): lax.all_gather(rrb, ('leaf', 'rows'), axis=1, tiled=True)  35.9 us
  transfers between devices with their start and end apart: 8, of which 8 were waited for; matrix products, arithmetic and copies ran while one was open for 0% of the time, Pallas kernels for 0%

commit v1 on v0

--- a/solution.py
+++ b/solution.py
@@ -72,7 +72,7 @@
     parent_mask = parent_pos < parent_height[0]
     pupd = jnp.where(parent_mask[None, :], pupd, 0.0)
     parent_root = jnp.zeros((rcount, root_width), jnp.float32).at[:, parent_rows[0]].add(pupd)
-    root_acc = root_from_leaves + lax.psum(parent_root, ("leaf", "rows"))
+    root_acc = root_from_leaves + lax.psum(lax.psum(parent_root, "leaf"), "rows")
     root_slice = lax.dynamic_slice_in_dim(root_acc, flat_index * root_cols, root_cols, 1)
     rrb = (root_rhs - root_slice).astype(jnp.bfloat16)
     block = root_inv

time: 917 us -> 880 us (0.960)
  waiting for transfers between devices: 681 us -> 644 us
    psum x2, waiting for transfers between devices: 182 us -> 146 us  [the longest x1 105 us: shards(): lax.psum(lax.psum(parent_root, 'leaf'), 'rows')]
where the time goes in v1:
time: 880 us
  waiting for transfers between devices  644 us (73%)
  blocking collectives  159 us (18%)
  local copies, waits for them, and re-layouts  35.5 us (4%)
  between operations  15 us (2%)
  matrix products  13.8 us (2%)
  other arithmetic  12.2 us (1%)
    unnamed x10, waiting for transfers between devices  153 us
    psum x1, waiting for transfers between devices, shards(): lax.psum(lax.psum(parent_root, 'leaf'), 'rows')  105 us
    psum x1, waiting for transfers between devices, shards(): group_acc = lax.psum(local_acc, 'rows')  101 us
    psum x1, waiting for transfers between devices, shards(): root_full = lax.psum(root_term, 'rows')  98.3 us
    reduce_scatter x1, waiting for transfers between devices, shards(): lax.psum_scatter(parent_sol_term, 'rows', scatter_dimension=1, tiled=True)  73.7 us
    reduce_scatter x1, waiting for transfers between devices, shards(): lax.psum_scatter(parent_term, 'rows', scatter_dimension=1, tiled=True)  71.9 us
    psum x1, waiting for transfers between devices, shards(): lax.psum(parent_root, 'leaf')  41.5 us
    all_gather x1, blocking collectives, shards(): lax.all_gather(rrb, ('leaf', 'rows'), axis=1, tiled=True)  36.4 us
  transfers between devices with their start and end apart: 8, of which 8 were waited for; matrix products, arithmetic and copies ran while one was open for 0% of the time, Pallas kernels for 0%

profile of v1, /device:TPU:0, one launch (start us, length us, event | category | flops | bytes accessed | tf_op | source)
XLA Modules:
  0.0 879.7 jit_solution(1502519760044363096)
XLA Ops:
  8.9 27.5 %all_gather.18 = bf16[8,4,2048]{0,1,2:T(4,128)(2,1)S(1)} all-gather(bf16[8,4,64]{0,1,2:T(4,128)(2,1)S(1)} %copy.62), channel_id=1, replica_groups=mesh['leaf'=4,'rows'=32] {'rows'}, dimensions={2}, use_global_device_ids=true | all-gather | bytes 135168 | tf_op jit(solution)/shard_map/all_gather | solution.py:33
  37.3 25.3 %all_gather.19 = bf16[8,4,2048]{0,1,2:T(4,128)(2,1)S(1)} all-gather(bf16[8,4,64]{0,1,2:T(4,128)(2,1)S(1)} %copy.64), channel_id=1, replica_groups=mesh['leaf'=4,'rows'=32] {'rows'}, dimensions={2}, use_global_device_ids=true | all-gather | bytes 135168 | tf_op jit(solution)/shard_map/all_gather | solution.py:41
  62.7 3.4 fusion.6
  66.3 8.2 scatter_custom_fusion
  74.5 3.5 copy.67
  78.9 100.7 %all-reduce.6.cloned.1.call-done = f32[8,8192]{1,0:T(8,128)} async-done(((f32[8,8192]{1,0:T(8,128)}), f32[8,8192]{1,0:T(8,128)}) %all-reduce.6.cloned.1.call-update) | async-done | bytes 262160 | tf_op jit(solution)/shard_map/psum | solution.py:54
  179.6 1.6 fusion.35
  181.2 24.6 %all_gather.20 = bf16[8,4096]{1,0:T(8,128)(2,1)S(1)} all-gather(bf16[8,128]{1,0:T(8,128)(2,1)S(1)} %subtract_convert_fusion.3), channel_id=1, replica_groups=mesh['leaf'=4,'rows'=32] {'rows'}, dimensions={1}, use_global_device_ids=true | all-gather | bytes 67584 | tf_op jit(solution)/shard_map/all_gather | solution.py:63
  206.2 21.5 %all_gather.21 = bf16[8,4096]{1,0:T(8,128)(2,1)S(1)} all-gather(bf16[8,128]{1,0:T(8,128)(2,1)S(1)} %get-tuple-element.24), channel_id=1, replica_groups=mesh['leaf'=4,'rows'=32] {'rows'}, dimensions={1}, use_global_device_ids=true | all-gather | bytes 67584 | tf_op jit(solution)/shard_map/all_gather | solution.py:69
  228.2 1.5 scatter_custom_fusion.1
  229.8 1.2 copy.69
  231.1 41.5 %all-reduce.12.cloned.1.call-done = (f32[8,4096]{1,0:T(8,128)}, f32[8,4096]{1,0:T(8,128)}) async-done(((f32[8,4096]{1,0:T(8,128)}, f32[8,4096]{1,0:T(8,128)}), (f32[8,4096]{1,0:T(8,128)}, f32[8,4096]{1,0:T(8,128)})) %all-reduce.12.cloned.1.call-update) | async-done | bytes 262160 | tf_op jit(solution)/shard_map/psum | solution.py:75
  272.6 104.8 %all-reduce.8.cloned.1.call-done = f32[8,4096]{1,0:T(8,128)} async-done(((f32[8,4096]{1,0:T(8,128)}), f32[8,4096]{1,0:T(8,128)}) %all-reduce.8.cloned.1.call-update) | async-done | bytes 131088 | tf_op jit(solution)/shard_map/psum | solution.py:75
  378.2 36.4 %all-gather = bf16[128,32,8]{1,2,0:T(8,128)(2,1)S(1)} all-gather(bf16[1,32,8]{1,2,0:T(8,128)(2,1)S(1)} %fusion.31), channel_id=1, replica_groups=mesh['leaf'=4,'rows'=32] {'leaf','rows'}, dimensions={0}, use_global_device_ids=true | all-gather | bytes 66048 | tf_op jit(solution)/shard_map/all_gather | solution.py:80
  415.0 3.2 fusion.13
  418.3 98.3 %all-reduce.10.cloned.1.call-done = f32[8,4096]{1,0:T(8,128)} async-done(((f32[8,4096]{1,0:T(8,128)}), f32[8,4096]{1,0:T(8,128)}) %all-reduce.10.cloned.1.call-update) | async-done | bytes 131088 | tf_op jit(solution)/shard_map/psum | solution.py:85
  517.5 1.3 copy.71
  518.8 2.0 gather_fusion
  520.8 1.0 fusion.14
  521.9 71.9 %reduce-scatter.9.cloned.1.call-done = f32[8,128]{1,0:T(8,128)} async-done(((f32[8,4096]{1,0:T(8,128)}), f32[8,128]{1,0:T(8,128)}) %reduce-scatter.9.cloned.1.call-update) | async-done | bytes 4112 | tf_op jit(solution)/shard_map/reduce_scatter | solution.py:91
  593.8 1.6 fusion.17
  595.5 73.7 %reduce-scatter.11.cloned.1.call-done = f32[8,128]{1,0:T(8,128)} async-done(((f32[8,4096]{1,0:T(8,128)}), f32[8,128]{1,0:T(8,128)}) %reduce-scatter.11.cloned.1.call-update) | async-done | bytes 4112 | tf_op jit(solution)/shard_map/reduce_scatter | solution.py:94
  669.9 23.5 %all_gather.23 = bf16[8,4096]{1,0:T(8,128)(2,1)S(1)} all-gather(bf16[8,128]{1,0:T(8,128)(2,1)S(1)} %convert_element_type.38), channel_id=1, replica_groups=mesh['leaf'=4,'rows'=32] {'rows'}, dimensions={1}, use_global_device_ids=true | all-gather | bytes 67584 | tf_op jit(solution)/shard_map/all_gather | solution.py:95
  694.5 3.2 gather_fusion.1
  697.8 2.8 convolution_bitcast_fusion.1
  700.6 3.1 copy.76
  703.7 4.5 reshape.143
  708.3 76.7 %reduce-scatter.13.cloned.1.call-done = f32[64,32]{1,0:T(8,128)} async-done(((f32[2048,32]{1,0:T(8,128)}), f32[64,32]{1,0:T(8,128)}) %reduce-scatter.13.cloned.1.call-update) | async-done | bytes 8208
  786.2 3.1 copy.78
  789.3 4.5 reshape.145
  793.9 1.4 constant_dynamic-slice_fusion
  795.2 76.0 %reduce-scatter.15.cloned.1.call-done = f32[64,32]{1,0:T(8,128)} async-done(((f32[2048,32]{1,0:T(8,128)}), f32[64,32]{1,0:T(8,128)}) %reduce-scatter.15.cloned.1.call-update) | async-done | bytes 8208
  (64 shorter events, 10.8 us)
Async XLA Ops:
  7.2 29.2 %copy-start = (bf16[4,64,2048]{2,1,0:T(8,128)(2,1)S(1)}, bf16[4,64,2048]{2,1,0:T(8,128)(2,1)}, u32[]{:S(2)}) copy-start(bf16[4,64,2048]{2,1,0:T(8,128)(2,1)} %param.15) | copy-start | bytes 3145732
  7.2 172.4 %all-reduce.6.cloned.1.call-start = ((), (), s32[]{:S(2)}) async-start(), calls=%async_computation.4 | async-start | bytes 524288 | tf_op jit(solution)/shard_map/psum | solution.py:54
  36.3 26.3 %copy-start.7 = (s32[4]{0:T(128)S(1)}, s32[4]{0:T(128)}, u32[]{:S(2)}) copy-start(s32[4]{0:T(128)} %param.18) | copy-start | bytes 52
  74.5 3.6 copy-start.8
  74.5 106.7 %copy-start.5 = (f32[8,1,128]{2,1,0:T(1,128)S(1)}, f32[8,1,128]{2,1,0:T(1,128)}, u32[]{:S(2)}) copy-start(f32[8,1,128]{2,1,0:T(1,128)} %param.13) | copy-start | bytes 12292
  74.5 131.4 %copy-start.3 = (bf16[1,128,4096]{2,1,0:T(8,128)(2,1)S(1)}, bf16[1,128,4096]{2,1,0:T(8,128)(2,1)}, u32[]{:S(2)}) copy-start(bf16[1,128,4096]{2,1,0:T(8,128)(2,1)} %param.19) | copy-start | bytes 3145732
  78.0 149.7 %copy-start.1 = (bf16[1,128,4096]{2,1,0:T(8,128)(2,1)S(1)}, bf16[1,128,4096]{2,1,0:T(8,128)(2,1)}, u32[]{:S(2)}) copy-start(bf16[1,128,4096]{2,1,0:T(8,128)(2,1)} %param.20) | copy-start | bytes 3145732
  78.1 194.5 %all-reduce.12.cloned.1.call-start = ((), (), s32[]{:S(2)}) async-start(), calls=%async_computation.11 | async-start | bytes 524288 | tf_op jit(solution)/shard_map/psum | solution.py:75
  228.2 149.3 %copy-start.6 = (f32[8,32]{1,0:T(8,128)S(1)}, f32[8,32]{1,0:T(8,128)}, u32[]{:S(2)}) copy-start(f32[8,32]{1,0:T(8,128)} %param.14) | copy-start | bytes 3076
  231.0 146.5 %all-reduce.8.cloned.1.call-start = ((), (), s32[]{:S(2)}) async-start(), calls=%async_computation.5 | async-start | bytes 262144 | tf_op jit(solution)/shard_map/psum | solution.py:75
  272.6 244.0 %all-reduce.10.cloned.1.call-start = ((), (), s32[]{:S(2)}) async-start(), calls=%async_computation.6 | async-start | bytes 262144 | tf_op jit(solution)/shard_map/psum | solution.py:85
  414.7 106.1 %copy-start.2 = (bf16[1,128,4096]{2,1,0:T(8,128)(2,1)S(1)}, bf16[1,128,4096]{2,1,0:T(8,128)(2,1)}, u32[]{:S(2)}) copy-start(bf16[1,128,4096]{2,1,0:T(8,128)(2,1)} %param.20) | copy-start | bytes 3145732
  415.0 178.8 %copy-start.4 = (bf16[1,128,4096]{2,1,0:T(8,128)(2,1)S(1)}, bf16[1,128,4096]{2,1,0:T(8,128)(2,1)}, u32[]{:S(2)}) copy-start(bf16[1,128,4096]{2,1,0:T(8,128)(2,1)} %param.19) | copy-start | bytes 3145732
  418.2 175.6 %reduce-scatter.9.cloned.1.call-start = ((), (), s32[]{:S(2)}) async-start(), calls=%async_computation.7 | async-start | bytes 135168 | tf_op jit(solution)/shard_map/reduce_scatter | solution.py:91
  521.9 147.3 %reduce-scatter.11.cloned.1.call-start = ((), (), s32[]{:S(2)}) async-start(), calls=%async_computation.8 | async-start | bytes 135168 | tf_op jit(solution)/shard_map/reduce_scatter | solution.py:94
  595.4 189.6 %reduce-scatter.13.cloned.1.call-start = ((), (), s32[]{:S(2)}) async-start(), calls=%async_computation.9 | async-start | bytes 1081344
  708.2 163.0 %reduce-scatter.15.cloned.1.call-start = ((), (), s32[]{:S(2)}) async-start(), calls=%async_computation.10 | async-start | bytes 1081344
Sparse Core Ops, SparseCore 0:
  78.2 101.3 all-reduce.5
  231.1 41.3 all-reduce.11
  275.8 101.6 all-reduce.7
  418.3 98.1 all-reduce.9
  522.0 71.7 reduce-scatter.8
  597.6 71.5 reduce-scatter.10
  708.4 76.6 reduce-scatter.12
  794.0 77.2 reduce-scatter.14
